TPU v7x, 32 devices: a whole 2x2x4 slice. The times are simulated.
32 devices in a mesh: groups: 2 (over x), dap: 16 (over z, y, core).
Axes of the slice: x: 2, y: 2, z: 4, core: 2. Of those that a mesh axis runs over, the one named last changes fastest.
Arguments:
- homolog_tensor: bfloat16 [128, 32, 256], P(('groups', 'dap')), parts along dimension 0, may hold values from -1 to 1
- couple_tensor: bfloat16 [64, 32, 128], P(('groups', 'dap')), parts along dimension 0, may hold values from -6 to 6
- horizontal_drop_filter: int32 [64, 256], P('groups'), parts along dimension 0, may hold values 0 or 1
- couple_offset_matrix: bfloat16 [128, 8], replicated, may hold values from -0.29882812 to 0.29882812
- horizontal_attend_matrix: bfloat16 [256, 1024], replicated, may hold values from -0.375 to 0.375
- horizontal_exit_matrix: bfloat16 [256, 256], replicated, may hold values from -0.375 to 0.375
- vertical_attend_matrix: bfloat16 [256, 1024], replicated, may hold values from -0.375 to 0.375
- vertical_exit_matrix: bfloat16 [256, 256], replicated, may hold values from -0.375 to 0.375
- averaged_product_flanks: bfloat16 [256, 64], replicated, may hold values from -0.375 to 0.375
- averaged_product_exit: bfloat16 [1024, 128], replicated, may hold values from -1 to 1
Outputs:
- alignment_output: bfloat16 [128, 32, 256], P('groups', 'dap'), parts along dimension 0
- pair_output_state: bfloat16 [64, 32, 128], P(('groups', 'dap')), parts along dimension 0
There are 2 independent parts, one for each index of `groups`. A program takes and returns all parts, laid end to end along the dimension named above; an argument that names none is the same for every part. Nothing has to cross between parts.
All inputs are finite; a program needn't handle non-finite values.
Results may differ from a plain program's by a relative error of at most 0.012.
Values may be sent and summed in bfloat16 or wider, within the bound.
No kernel may reach another device: no remote copies, remote signals or barrier semaphores. Data moves between devices by JAX's collectives and lax.ppermute only.
A program may use at most 64 MiB of HBM per device.

v0:
```python
import jax
import jax.numpy as jnp
from jax import lax
from jax.sharding import PartitionSpec as P

HEAD_NUMBER = 8
HEAD_WIDTH = 32
FACTOR_FEATURES = 32


def standardise_features(values):
    values = values.astype(jnp.float32)
    center = values - jnp.mean(values, axis=-1, keepdims=True)
    spread = jnp.mean(center * center, axis=-1, keepdims=True)
    return center * lax.rsqrt(spread + 1e-05)


def attend(normed, w_qkvg, w_out, bias):
    batch, length = (normed.shape[0], normed.shape[1])
    proj = jnp.einsum("blc,cf->blf", normed, w_qkvg, preferred_element_type=jnp.float32)
    proj = proj.reshape(batch, length, 4, HEAD_NUMBER, HEAD_WIDTH)
    query = (proj[:, :, 0] * HEAD_WIDTH ** (-0.5)).astype(jnp.bfloat16)
    keys = proj[:, :, 1].astype(jnp.bfloat16)
    values = proj[:, :, 2].astype(jnp.bfloat16)
    gate = proj[:, :, 3]
    if bias is None:
        bias = jnp.zeros((HEAD_NUMBER, length, length), jnp.bfloat16)

    def one_head(items):
        qh, kh, vh, bh = items
        scores = jnp.einsum("bid,bjd->bij", qh, kh, preferred_element_type=jnp.float32)
        scores = scores + bh.astype(jnp.float32)[None]
        weights = jax.nn.softmax(scores, axis=-1).astype(jnp.bfloat16)
        return jnp.einsum("bij,bjd->bid", weights, vh, preferred_element_type=jnp.float32)

    heads = lax.map(
        one_head,
        (jnp.moveaxis(query, 2, 0), jnp.moveaxis(keys, 2, 0), jnp.moveaxis(values, 2, 0), bias),
    )
    heads = jnp.moveaxis(heads, 0, 2)
    gated = (
        (jax.nn.sigmoid(gate) * heads)
        .astype(jnp.bfloat16)
        .reshape(batch, length, HEAD_NUMBER * HEAD_WIDTH)
    )
    return jnp.einsum("blk,kc->blc", gated, w_out, preferred_element_type=jnp.float32)


def shards(
    homolog_tensor,
    couple_tensor,
    horizontal_drop_filter,
    couple_offset_matrix,
    horizontal_attend_matrix,
    horizontal_exit_matrix,
    vertical_attend_matrix,
    vertical_exit_matrix,
    averaged_product_flanks,
    averaged_product_exit,
):
    normed_pair = standardise_features(couple_tensor).astype(jnp.bfloat16)
    own_bias = jnp.einsum(
        "ijz,zh->hij", normed_pair, couple_offset_matrix, preferred_element_type=jnp.float32
    ).astype(jnp.bfloat16)
    bias = lax.all_gather(own_bias, "dap", axis=1, tiled=True)
    starting_answer = standardise_features(homolog_tensor).astype(jnp.bfloat16)
    perform_refresh = attend(
        starting_answer, horizontal_attend_matrix, horizontal_exit_matrix, bias
    )
    homolog_later = (
        homolog_tensor.astype(jnp.float32)
        + horizontal_drop_filter.astype(jnp.float32) * (1.0 / 0.9) * perform_refresh
    ).astype(jnp.bfloat16)
    incoming_blocks = lax.all_to_all(homolog_later, "dap", split_axis=1, concat_axis=0, tiled=True)
    column_layout = jnp.swapaxes(incoming_blocks, 0, 1)
    perform_refresh = attend(
        standardise_features(column_layout).astype(jnp.bfloat16),
        vertical_attend_matrix,
        vertical_exit_matrix,
        None,
    )
    alignment_output = jnp.swapaxes(
        (column_layout.astype(jnp.float32) + perform_refresh).astype(jnp.bfloat16), 0, 1
    )
    final_result = standardise_features(alignment_output).astype(jnp.bfloat16)
    factors = jnp.einsum(
        "sic,cf->sif", final_result, averaged_product_flanks, preferred_element_type=jnp.float32
    )
    left = factors[..., :FACTOR_FEATURES].astype(jnp.bfloat16)
    right = factors[..., FACTOR_FEATURES:].astype(jnp.bfloat16)
    total = left.shape[0]
    own_rows = left.shape[1]
    whole = lax.all_gather(right, "dap", axis=1, tiled=True)
    outer = jnp.einsum("sic,sjd->ijcd", left, whole, preferred_element_type=jnp.float32) / total
    outer = outer.astype(jnp.bfloat16).reshape(
        own_rows, whole.shape[1], FACTOR_FEATURES * FACTOR_FEATURES
    )
    change = jnp.einsum(
        "ijk,kz->ijz", outer, averaged_product_exit, preferred_element_type=jnp.float32
    )
    pair_output_state = (couple_tensor.astype(jnp.float32) + change).astype(jnp.bfloat16)
    return (alignment_output, pair_output_state)


def solution(mesh):
    placed = (
        P(("groups", "dap"), None, None),
        P(("groups", "dap"), None, None),
        P("groups", None),
        P(),
        P(),
        P(),
        P(),
        P(),
        P(),
        P(),
    )
    return jax.shard_map(
        shards,
        mesh=mesh,
        in_specs=placed,
        out_specs=(P("groups", "dap", None), P(("groups", "dap"), None, None)),
        check_vma=False,
    )
```

profile of v0, /device:TPU:0, one launch (start us, length us, event | category | flops | bytes accessed | tf_op | source)
XLA Modules:
  0.0 80.2 jit_solution(14656866743398978957)
XLA Ops:
  0.6 1.0 %convert_reduce_fusion = f32[4,32]{1,0:T(4,128)S(1)} fusion(bf16[4,32,256]{2,1,0:T(8,128)(2,1)} %param.14), kind=kLoop, calls=%fused_computation.81 | loop fusion | flops 65408 | bytes 66048 | tf_op jit(solution)/shard_map/reduce_sum | solution.py:13
  1.7 1.0 %fusion.104 = f32[4,32]{1,0:T(4,128)S(1)} fusion(bf16[4,32,256]{2,1,0:T(8,128)(2,1)} %param.14, f32[4,32]{1,0:T(4,128)S(1)} %broadcast_multiply_fusion), kind=kLoop, calls=%fused_computation.88 | loop fusion | flops 130944 | bytes 66560 | tf_op jit(solution)/shard_map/reduce_sum | solution.py:14
  2.7 1.1 %fusion.87 = f32[4,32,1024]{2,1,0:T(8,128)S(1)} fusion(bf16[256,1024]{1,0:T(8,128)(2,1)S(1)} %copy-done, bf16[4,32,256]{2,1,0:T(8,128)(2,1)} %param.14, f32[4,32]{1,0:T(4,128)S(1)} %add_rsqrt_fusion, f32[4,32]{1,0:T(4,128)S(1)} %broadcast_multiply_fusion), kind=kOutput, calls=%fused_computation.63 | convolution fusion | flops 67239936 | bytes 1115136 | tf_op jit(solution)/shard_map/blc,cf->blf/dot_general | solution.py:20
  3.8 0.7 reshape.102
  4.5 2.6 %copy.41 = f32[4,32,4,8,32]{4,1,0,3,2:T(8,128)} copy(f32[4,32,4,8,32]{4,3,2,1,0:T(8,128)S(1)} %reshape.102) | data formatting | bytes 1048576 | tf_op jit(solution)/shard_map/reshape | solution.py:21
  7.1 2.2 %copy.76 = bf16[4,32,4,8,32]{4,1,0,3,2:T(8,128)(2,1)} copy(f32[4,32,4,8,32]{4,3,2,1,0:T(8,128)S(1)} %reshape.102) | data formatting | bytes 786432 | tf_op jit(solution)/shard_map/reshape | solution.py:21
  9.3 1.1 %fusion.90 = bf16[8,4,32,32]{3,2,1,0:T(8,128)(2,1)S(1)} fusion(f32[4,32,4,8,32]{4,1,0,3,2:T(8,128)} %copy.41), kind=kLoop, calls=%fused_computation.66 | loop fusion | flops 65536 | bytes 196608 | tf_op jit(solution)/shard_map/transpose | solution.py:38
  10.4 1.1 %slice_bitcast_fusion = (bf16[8,4,32,32]{3,2,1,0:T(8,128)(2,1)S(1)}, bf16[8,4,32,32]{3,2,1,0:T(8,128)(2,1)S(1)}) fusion(bf16[4,32,4,8,32]{4,1,0,3,2:T(8,128)(2,1)} %copy.76), kind=kLoop, calls=%fused_computation.75 | loop fusion | bytes 262144 | tf_op jit(solution)/shard_map/transpose | solution.py:38
  11.9 23.3 %all_gather.6 = bf16[8,32,32]{2,0,1:T(8,128)(2,1)S(1)} all-gather(bf16[8,2,32]{2,0,1:T(8,128)(2,1)S(1)} %fusion.78), channel_id=1, replica_groups=mesh['groups'=2,'dap'=16] {'dap'}, dimensions={1}, use_global_device_ids=true | all-gather | bytes 17408 | tf_op jit(solution)/shard_map/all_gather | solution.py:65
  35.4 4.3 %while.20 = (s32[]{:T(128)}, f32[8,4,32,32]{3,2,1,0:T(8,128)S(1)}, bf16[8,4,32,32]{3,2,1,0:T(8,128)(2,1)S(1)}, bf16[8,4,32,32]{3,2,1,0:T(8,128)(2,1)S(1)}, bf16[...) while((s32[]{:T(128)}, f32[8,4,32,32]{3,2,1,0:T(8,128)S(1)}, ...), condition=%wide.region_7.8_spmd, body=%wide.region_4.7_spmd.sunk | while | flops 816320 | bytes 274001 | solution.py:36
  39.7 1.3 %fusion.89 = bf16[4,32,8,32]{3,1,0,2:T(8,128)(2,1)S(1)} fusion(f32[8,4,32,32]{3,2,1,0:T(8,128)S(1)} %get-tuple-element.61, f32[4,32,4,8,32]{4,1,0,3,2:T(8,128)} %copy.41), kind=kLoop, calls=%fused_computation.65 | loop fusion | flops 163840 | bytes 327680 | tf_op jit(solution)/shard_map/convert_element_type | solution.py:43
  41.5 0.7 copy.46
  42.2 3.5 %all-to-all-start = ((bf16[4,32,256]{2,0,1:T(4,128)(2,1)}), bf16[4,32,256]{2,0,1:T(4,128)(2,1)S(1)}, u32[]{:S(2)}, u32[]{:S(2)}) async-start(bf16[4,32,256]{2,0,1:T(4,128)(2,1)} %copy.46), calls=%async_computation | async-start | bytes 131072 | tf_op jit(solution)/shard_map/all_to_all | solution.py:74
  45.7 6.8 %all-to-all-done = bf16[4,32,256]{2,0,1:T(4,128)(2,1)S(1)} async-done(((bf16[4,32,256]{2,0,1:T(4,128)(2,1)}), bf16[4,32,256]{2,0,1:T(4,128)(2,1)S(1)}, u32[]{:S(2)}, u32[]{:S(2)}) %all-to-all-start) | async-done | bytes 65568 | tf_op jit(solution)/shard_map/all_to_all | solution.py:74
  52.9 0.4 fusion.85
  53.5 4.7 %while.21 = (s32[]{:T(128)}, f32[8,2,64,32]{2,3,0,1:T(8,128)S(1)}, bf16[8,2,64,32]{2,3,0,1:T(8,128)(2,1)S(1)}, bf16[8,2,64,32]{2,3,0,1:T(8,128)(2,1)S(1)}, bf16[8,2,64,32]{2,3,0,1:T(8,128)(2,1)S(1)}, /*index=5*/s32[]{:T(128)}) while((s32[]{:T(128)}, f32[8,2,64,32]{2,3,0,1:T(8,128)S(1)}, bf16[8,2,64,32]{2,3,0,1:T(8,128)(2,1)S(1)}, ...), condition=%wide.region_13.14_spmd, body=%wide.region_10.13_spmd.sunk | while | flops 1614080 | bytes 119365 | solution.py:36
  53.8 0.3 fusion.169
  54.4 0.3 fusion.169
  55.0 0.3 fusion.169
  55.6 0.3 fusion.169
  58.7 0.7 copy.55
  59.8 18.5 %all_gather.7 = bf16[64,32,32]{0,2,1:T(8,128)(2,1)S(1)} all-gather(bf16[64,2,32]{0,2,1:T(8,128)(2,1)S(1)} %slice.54), channel_id=1, replica_groups=mesh['groups'=2,'dap'=16] {'dap'}, dimensions={1}, use_global_device_ids=true | all-gather | bytes 139264 | tf_op jit(solution)/shard_map/all_gather | solution.py:93
  78.9 0.5 reshape.106
  79.5 0.8 fusion.77
  (88 shorter events, 10.6 us)
Async XLA Ops:
  0.6 2.0 %copy-start = (bf16[256,1024]{1,0:T(8,128)(2,1)S(1)}, bf16[256,1024]{1,0:T(8,128)(2,1)}, u32[]{:S(2)}) copy-start(bf16[256,1024]{1,0:T(8,128)(2,1)} %param.18) | copy-start | bytes 1572868
  7.1 4.4 %copy-start.4 = (bf16[2,32,128]{2,1,0:T(8,128)(2,1)S(1)}, bf16[2,32,128]{2,1,0:T(8,128)(2,1)}, u32[]{:S(2)}) copy-start(bf16[2,32,128]{2,1,0:T(8,128)(2,1)} %param.15) | copy-start | bytes 49156
  7.1 4.7 %copy-start.9 = (bf16[128,8]{0,1:T(8,128)(2,1)S(1)}, bf16[128,8]{0,1:T(8,128)(2,1)}, u32[]{:S(2)}) copy-start(bf16[128,8]{0,1:T(8,128)(2,1)} %param.17) | copy-start | bytes 6148
  35.4 5.9 %copy-start.7 = (s32[32,256]{1,0:T(8,128)S(1)}, s32[32,256]{1,0:T(8,128)}, u32[]{:S(2)}) copy-start(s32[32,256]{1,0:T(8,128)} %param.16) | copy-start | bytes 98308
  35.4 5.9 %copy-start.1 = (bf16[4,32,256]{2,1,0:T(8,128)(2,1)S(1)}, bf16[4,32,256]{2,1,0:T(8,128)(2,1)}, u32[]{:S(2)}) copy-start(bf16[4,32,256]{2,1,0:T(8,128)(2,1)} %param.14) | copy-start | bytes 196612
  35.4 5.9 %copy-start.6 = (bf16[256,256]{1,0:T(8,128)(2,1)S(1)}, bf16[256,256]{1,0:T(8,128)(2,1)}, u32[]{:S(2)}) copy-start(bf16[256,256]{1,0:T(8,128)(2,1)} %param.19) | copy-start | bytes 393220
  39.7 13.2 %copy-start.2 = (bf16[256,1024]{1,0:T(8,128)(2,1)S(1)}, bf16[256,1024]{1,0:T(8,128)(2,1)}, u32[]{:S(2)}) copy-start(bf16[256,1024]{1,0:T(8,128)(2,1)} %param.20) | copy-start | bytes 1572868
  42.2 10.4 %all-to-all-start = ((bf16[4,32,256]{2,0,1:T(4,128)(2,1)}), bf16[4,32,256]{2,0,1:T(4,128)(2,1)S(1)}, u32[]{:S(2)}, u32[]{:S(2)}) async-start(bf16[4,32,256]{2,0,1:T(4,128)(2,1)} %copy.46), calls=%async_computation | async-start | bytes 131072 | tf_op jit(solution)/shard_map/all_to_all | solution.py:74
  53.4 4.9 %copy-start.5 = (bf16[256,256]{1,0:T(8,128)(2,1)S(1)}, bf16[256,256]{1,0:T(8,128)(2,1)}, u32[]{:S(2)}) copy-start(bf16[256,256]{1,0:T(8,128)(2,1)} %param.21) | copy-start | bytes 393220
  53.5 6.1 %copy-start.8 = (bf16[256,64]{0,1:T(8,128)(2,1)S(1)}, bf16[256,64]{0,1:T(8,128)(2,1)}, u32[]{:S(2)}) copy-start(bf16[256,64]{0,1:T(8,128)(2,1)} %param.22) | copy-start | bytes 98308
  58.3 21.2 %copy-start.3 = (bf16[1024,128]{1,0:T(8,128)(2,1)S(1)}, bf16[1024,128]{1,0:T(8,128)(2,1)}, u32[]{:S(2)}) copy-start(bf16[1024,128]{1,0:T(8,128)(2,1)} %param.23) | copy-start | bytes 786436
where the time goes:
time: 80.6 us; the launch traced here: 80.2 us
  blocking collectives  41.8 us (52%)
  matrix products  12.4 us (15%)
  local copies, waits for them, and re-layouts  9.33 us (12%)
  waiting for transfers between devices  6.85 us (8%)
  other arithmetic  5.33 us (7%)
  starting transfers between devices  3.5 us (4%)
  between operations  0.95 us (1%)
    all_gather x1, blocking collectives, shards(): bias = lax.all_gather(own_bias, 'dap', axis=1, tiled=True)  23.3 us
    all_gather x1, blocking collectives, shards(): whole = lax.all_gather(right, 'dap', axis=1, tiled=True)  18.5 us
    all_to_all x1, waiting for transfers between devices, shards(): lax.all_to_all(homolog_later, 'dap', split_axis=1, concat_axis=0, tiled=T...  6.85 us
    dot_general x16, matrix products, one_head(): jnp.einsum('bij,bjd->bid', weights, vh, preferred_element_type=jnp.float32)  5.53 us
    reshape x3, local copies, waits for them, and re-layouts, attend(): proj = proj.reshape(batch, length, 4, HEAD_NUMBER, HEAD_WIDTH)  5.46 us
    all_to_all x1, starting transfers between devices, shards(): lax.all_to_all(homolog_later, 'dap', split_axis=1, concat_axis=0, tiled=T...  3.5 us
    sub x16, matrix products, one_head(): weights = jax.nn.softmax(scores, axis=-1).astype(jnp.bfloat16)  3.4 us
  transfers between devices with their start and end apart: 1, of which 1 were waited for; matrix products, arithmetic and copies ran while one was open for 0% of the time, Pallas kernels for 0%

commit v1 on v0

--- a/solution.py
+++ b/solution.py
@@ -71,7 +71,16 @@
         homolog_tensor.astype(jnp.float32)
         + horizontal_drop_filter.astype(jnp.float32) * (1.0 / 0.9) * perform_refresh
     ).astype(jnp.bfloat16)
-    incoming_blocks = lax.all_to_all(homolog_later, "dap", split_axis=1, concat_axis=0, tiled=True)
+    state_the_files = lambda field: jnp.concatenate(
+        lax.all_to_all(
+            jnp.stack(jnp.split(field, lax.psum(1, "dap"), axis=1), 0),
+            "dap",
+            concat_axis=0,
+            split_axis=0,
+        ),
+        0,
+    )
+    incoming_blocks = state_the_files(homolog_later)
     column_layout = jnp.swapaxes(incoming_blocks, 0, 1)
     perform_refresh = attend(
         standardise_features(column_layout).astype(jnp.bfloat16),

time: 80.6 us -> 89.4 us (1.11)
  local copies, waits for them, and re-layouts: 9.33 us -> 18.2 us
    unnamed x21 -> x36, local copies, waits for them, and re-layouts: 0.76 us -> 9.74 us
where the time goes in v1:
time: 89.4 us; the launch traced here: 89 us
  blocking collectives  41.7 us (47%)
  local copies, waits for them, and re-layouts  18.2 us (20%)
  matrix products  12.4 us (14%)
  waiting for transfers between devices  6.85 us (8%)
  other arithmetic  5.36 us (6%)
  starting transfers between devices  3.5 us (4%)
  between operations  0.95 us (1%)
    all_gather x1, blocking collectives, shards(): bias = lax.all_gather(own_bias, 'dap', axis=1, tiled=True)  23.3 us
    all_gather x1, blocking collectives, shards(): whole = lax.all_gather(right, 'dap', axis=1, tiled=True)  18.4 us
    unnamed x36, local copies, waits for them, and re-layouts  9.74 us
    all_to_all x1, waiting for transfers between devices, shards(): lax.all_to_all(jnp.stack(jnp.split(field, lax.psum(1, 'dap'), axis=1), 0)...  6.85 us
    dot_general x16, matrix products, one_head(): jnp.einsum('bij,bjd->bid', weights, vh, preferred_element_type=jnp.float32)  5.53 us
    reshape x3, local copies, waits for them, and re-layouts, attend(): proj = proj.reshape(batch, length, 4, HEAD_NUMBER, HEAD_WIDTH)  5.46 us
    all_to_all x1, starting transfers between devices, shards(): lax.all_to_all(jnp.stack(jnp.split(field, lax.psum(1, 'dap'), axis=1), 0)...  3.5 us
    sub x16, matrix products, one_head(): weights = jax.nn.softmax(scores, axis=-1).astype(jnp.bfloat16)  3.4 us
  transfers between devices with their start and end apart: 1, of which 1 were waited for; matrix products, arithmetic and copies ran while one was open for 0% of the time, Pallas kernels for 0%

profile of v1, /device:TPU:0, one launch (start us, length us, event | category | flops | bytes accessed | tf_op | source)
XLA Modules:
  0.0 89.0 jit_solution(15391860364701758695)
XLA Ops:
  0.6 1.0 %convert_reduce_fusion = f32[4,32]{1,0:T(4,128)S(1)} fusion(bf16[4,32,256]{2,1,0:T(8,128)(2,1)} %param.14), kind=kLoop, calls=%fused_computation.81 | loop fusion | flops 65408 | bytes 66048 | tf_op jit(solution)/shard_map/reduce_sum | solution.py:13
  1.7 1.0 %fusion.104 = f32[4,32]{1,0:T(4,128)S(1)} fusion(bf16[4,32,256]{2,1,0:T(8,128)(2,1)} %param.14, f32[4,32]{1,0:T(4,128)S(1)} %broadcast_multiply_fusion), kind=kLoop, calls=%fused_computation.88 | loop fusion | flops 130944 | bytes 66560 | tf_op jit(solution)/shard_map/reduce_sum | solution.py:14
  2.7 1.1 %fusion.87 = f32[4,32,1024]{2,1,0:T(8,128)S(1)} fusion(bf16[256,1024]{1,0:T(8,128)(2,1)S(1)} %copy-done, bf16[4,32,256]{2,1,0:T(8,128)(2,1)} %param.14, f32[4,32]{1,0:T(4,128)S(1)} %add_rsqrt_fusion, f32[4,32]{1,0:T(4,128)S(1)} %broadcast_multiply_fusion), kind=kOutput, calls=%fused_computation.63 | convolution fusion | flops 67239936 | bytes 1115136 | tf_op jit(solution)/shard_map/blc,cf->blf/dot_general | solution.py:20
  3.8 0.7 reshape.99
  4.5 2.6 %copy.43 = f32[4,32,4,8,32]{4,1,0,3,2:T(8,128)} copy(f32[4,32,4,8,32]{4,3,2,1,0:T(8,128)S(1)} %reshape.99) | data formatting | bytes 1048576 | tf_op jit(solution)/shard_map/reshape | solution.py:21
  7.1 2.2 %copy.82 = bf16[4,32,4,8,32]{4,1,0,3,2:T(8,128)(2,1)} copy(f32[4,32,4,8,32]{4,3,2,1,0:T(8,128)S(1)} %reshape.99) | data formatting | bytes 786432 | tf_op jit(solution)/shard_map/reshape | solution.py:21
  9.3 1.1 %fusion.90 = bf16[8,4,32,32]{3,2,1,0:T(8,128)(2,1)S(1)} fusion(f32[4,32,4,8,32]{4,1,0,3,2:T(8,128)} %copy.43), kind=kLoop, calls=%fused_computation.66 | loop fusion | flops 65536 | bytes 196608 | tf_op jit(solution)/shard_map/transpose | solution.py:38
  10.4 1.1 %slice_bitcast_fusion = (bf16[8,4,32,32]{3,2,1,0:T(8,128)(2,1)S(1)}, bf16[8,4,32,32]{3,2,1,0:T(8,128)(2,1)S(1)}) fusion(bf16[4,32,4,8,32]{4,1,0,3,2:T(8,128)(2,1)} %copy.82), kind=kLoop, calls=%fused_computation.75 | loop fusion | bytes 262144 | tf_op jit(solution)/shard_map/transpose | solution.py:38
  11.9 23.3 %all_gather.6 = bf16[8,32,32]{2,0,1:T(8,128)(2,1)S(1)} all-gather(bf16[8,2,32]{2,0,1:T(8,128)(2,1)S(1)} %fusion.78), channel_id=1, replica_groups=mesh['groups'=2,'dap'=16] {'dap'}, dimensions={1}, use_global_device_ids=true | all-gather | bytes 17408 | tf_op jit(solution)/shard_map/all_gather | solution.py:65
  35.4 4.3 %while.20 = (s32[]{:T(128)}, f32[8,4,32,32]{3,2,1,0:T(8,128)S(1)}, bf16[8,4,32,32]{3,2,1,0:T(8,128)(2,1)S(1)}, bf16[8,4,32,32]{3,2,1,0:T(8,128)(2,1)S(1)}, bf16[...) while((s32[]{:T(128)}, f32[8,4,32,32]{3,2,1,0:T(8,128)S(1)}, ...), condition=%wide.region_7.8_spmd, body=%wide.region_4.7_spmd.sunk | while | flops 816320 | bytes 274001 | solution.py:36
  39.7 1.3 %fusion.89 = bf16[4,32,8,32]{3,1,0,2:T(8,128)(2,1)S(1)} fusion(f32[8,4,32,32]{3,2,1,0:T(8,128)S(1)} %get-tuple-element.61, f32[4,32,4,8,32]{4,1,0,3,2:T(8,128)} %copy.43), kind=kLoop, calls=%fused_computation.65 | loop fusion | flops 163840 | bytes 327680 | tf_op jit(solution)/shard_map/convert_element_type | solution.py:43
  41.5 0.6 constant_dynamic-update-slice_fusion.15
  42.1 0.6 constant_dynamic-update-slice_fusion.14
  42.7 0.6 constant_dynamic-update-slice_fusion.13
  43.3 0.6 constant_dynamic-update-slice_fusion.12
  46.9 0.6 constant_dynamic-update-slice_fusion.6
  47.5 0.6 constant_dynamic-update-slice_fusion.5
  48.1 0.6 constant_dynamic-update-slice_fusion.4
  51.1 3.5 %all-to-all-start = ((bf16[16,4,2,256]{3,2,1,0:T(2,128)(2,1)}), bf16[16,4,2,256]{3,2,1,0:T(2,128)(2,1)S(1)}, u32[]{:S(2)}, u32[]{:S(2)}) async-start(bf16[16,4,2,256]{3,2,1,0:T(2,128)(2,1)} %constant_dynamic-update-slice_fusion), calls=%async_computation | async-start | bytes 131072 | tf_op jit(solution)/shard_map/all_to_all | solution.py:75
  54.6 6.8 %all-to-all-done = bf16[16,4,2,256]{3,2,1,0:T(2,128)(2,1)S(1)} async-done(((bf16[16,4,2,256]{3,2,1,0:T(2,128)(2,1)}), bf16[16,4,2,256]{3,2,1,0:T(2,128)(2,1)S(1)}, u32[]{:S(2)}, u32[]{:S(2)}) %all-to-all-start) | async-done | bytes 65568 | tf_op jit(solution)/shard_map/all_to_all | solution.py:75
  62.4 4.7 %while.21 = (s32[]{:T(128)}, f32[8,2,64,32]{2,3,0,1:T(8,128)S(1)}, bf16[8,2,64,32]{2,3,0,1:T(8,128)(2,1)S(1)}, bf16[8,2,64,32]{2,3,0,1:T(8,128)(2,1)S(1)}, bf16[8,2,64,32]{2,3,0,1:T(8,128)(2,1)S(1)}, /*index=5*/s32[]{:T(128)}) while((s32[]{:T(128)}, f32[8,2,64,32]{2,3,0,1:T(8,128)S(1)}, bf16[8,2,64,32]{2,3,0,1:T(8,128)(2,1)S(1)}, ...), condition=%wide.region_13.14_spmd, body=%wide.region_10.13_spmd.sunk | while | flops 1614080 | bytes 119365 | solution.py:36
  67.6 0.7 copy.57
  68.7 18.4 %all_gather.7 = bf16[64,32,32]{0,2,1:T(8,128)(2,1)S(1)} all-gather(bf16[64,2,32]{0,2,1:T(8,128)(2,1)S(1)} %slice.54), channel_id=1, replica_groups=mesh['groups'=2,'dap'=16] {'dap'}, dimensions={1}, use_global_device_ids=true | all-gather | bytes 139264 | tf_op jit(solution)/shard_map/all_gather | solution.py:102
  88.3 0.8 fusion.77
  (102 shorter events, 18.3 us)
Async XLA Ops:
  0.6 2.0 %copy-start = (bf16[256,1024]{1,0:T(8,128)(2,1)S(1)}, bf16[256,1024]{1,0:T(8,128)(2,1)}, u32[]{:S(2)}) copy-start(bf16[256,1024]{1,0:T(8,128)(2,1)} %param.18) | copy-start | bytes 1572868
  7.1 4.4 %copy-start.4 = (bf16[2,32,128]{2,1,0:T(8,128)(2,1)S(1)}, bf16[2,32,128]{2,1,0:T(8,128)(2,1)}, u32[]{:S(2)}) copy-start(bf16[2,32,128]{2,1,0:T(8,128)(2,1)} %param.15) | copy-start | bytes 49156
  7.1 4.7 %copy-start.9 = (bf16[128,8]{0,1:T(8,128)(2,1)S(1)}, bf16[128,8]{0,1:T(8,128)(2,1)}, u32[]{:S(2)}) copy-start(bf16[128,8]{0,1:T(8,128)(2,1)} %param.17) | copy-start | bytes 6148
  35.4 5.9 %copy-start.7 = (s32[32,256]{1,0:T(8,128)S(1)}, s32[32,256]{1,0:T(8,128)}, u32[]{:S(2)}) copy-start(s32[32,256]{1,0:T(8,128)} %param.16) | copy-start | bytes 98308
  35.4 5.9 %copy-start.1 = (bf16[4,32,256]{2,1,0:T(8,128)(2,1)S(1)}, bf16[4,32,256]{2,1,0:T(8,128)(2,1)}, u32[]{:S(2)}) copy-start(bf16[4,32,256]{2,1,0:T(8,128)(2,1)} %param.14) | copy-start | bytes 196612
  35.4 5.9 %copy-start.6 = (bf16[256,256]{1,0:T(8,128)(2,1)S(1)}, bf16[256,256]{1,0:T(8,128)(2,1)}, u32[]{:S(2)}) copy-start(bf16[256,256]{1,0:T(8,128)(2,1)} %param.19) | copy-start | bytes 393220
  39.7 22.1 %copy-start.2 = (bf16[256,1024]{1,0:T(8,128)(2,1)S(1)}, bf16[256,1024]{1,0:T(8,128)(2,1)}, u32[]{:S(2)}) copy-start(bf16[256,1024]{1,0:T(8,128)(2,1)} %param.20) | copy-start | bytes 1572868
  51.1 10.4 %all-to-all-start = ((bf16[16,4,2,256]{3,2,1,0:T(2,128)(2,1)}), bf16[16,4,2,256]{3,2,1,0:T(2,128)(2,1)S(1)}, u32[]{:S(2)}, u32[]{:S(2)}) async-start(bf16[16,4,2,256]{3,2,1,0:T(2,128)(2,1)} %constant_dynamic-update-slice_fusion), calls=%async_computation | async-start | bytes 131072 | tf_op jit(solution)/shard_map/all_to_all | solution.py:75
  62.3 4.9 %copy-start.5 = (bf16[256,256]{1,0:T(8,128)(2,1)S(1)}, bf16[256,256]{1,0:T(8,128)(2,1)}, u32[]{:S(2)}) copy-start(bf16[256,256]{1,0:T(8,128)(2,1)} %param.21) | copy-start | bytes 393220
  62.4 6.1 %copy-start.8 = (bf16[256,64]{0,1:T(8,128)(2,1)S(1)}, bf16[256,64]{0,1:T(8,128)(2,1)}, u32[]{:S(2)}) copy-start(bf16[256,64]{0,1:T(8,128)(2,1)} %param.22) | copy-start | bytes 98308
  67.2 21.1 %copy-start.3 = (bf16[1024,128]{1,0:T(8,128)(2,1)S(1)}, bf16[1024,128]{1,0:T(8,128)(2,1)}, u32[]{:S(2)}) copy-start(bf16[1024,128]{1,0:T(8,128)(2,1)} %param.23) | copy-start | bytes 786436
